TPU v7x, 512 devices: a whole 4x4x16 slice. The times are simulated.
512 devices in a mesh: rows: 64 (over y, z_lo, core), feat: 8 (over x, z_hi).
Axes of the slice: x: 4, y: 4, z: 16 (z_hi: 2, z_lo: 8; z = z_hi * 8 + z_lo), core: 2. Of those that a mesh axis runs over, the one named last changes fastest.
Arguments:
- logits: float32 [196608, 32], P('rows'), may hold values from -6 to 6
- labels: int32 [196608], P('rows'), may hold values from 0 to 31
- node_ids: int32 [196608], P('rows'), may hold values from 0 to 7
- bin_codes: int32 [196608, 256], P('rows', 'feat'), may hold values from 0 to 63
- split_feature: int32 [8], replicated, may hold values from 0 to 255
- split_bin: int32 [8], replicated, may hold values from 1 to 63
- split_missing: int32 [8], replicated, may hold values from 0 to 1
Outputs:
- new_logits: float32 [196608, 32], P('rows')
- gain_table: float32 [64, 32, 128], P('rows', 'feat')
- leaves: float32 [8, 2, 32], replicated
Inputs may be any that keep to these rules, and one draw needn't show every extreme that they name: `split_missing`: 1 sends the missing code 64 - 1 to the left child, 0 to the right child.
All inputs are finite; a program needn't handle non-finite values.
Results may differ from a plain program's by a relative error of at most 0.0014.
Values sent between devices are 32-bit elements; how exact they have to be, the bound alone decides.
A program may use at most 64 MiB of HBM per device.

v0:
```python
import math
import jax
import jax.numpy as jnp
from jax import lax
from jax.sharding import PartitionSpec as P

BINS = 64
reg_lambda = 1.0
step_size = 0.3


def split_score(sums, classes):
    grad_part = sums[..., :classes]
    hess_part = sums[..., classes:]
    return jnp.sum(grad_part * grad_part / (hess_part + reg_lambda), axis=-1)


def local(logits, labels, node_ids, bin_codes, split_feature, split_bin, split_missing):
    rows_dev, classes = logits.shape
    feats_dev = bin_codes.shape[1]
    node_count = split_feature.shape[0]
    bin_count = BINS
    per_node = lax.axis_size("rows") // node_count
    pairs_dev = feats_dev // per_node
    feat_pairs = feats_dev // 2
    width = 2 * classes
    expo_vals = jnp.exp(logits)
    soft_prob = expo_vals / jnp.sum(expo_vals, axis=1, keepdims=True)
    class_iota = jnp.arange(classes, dtype=jnp.int32)
    target = (labels[:, None] == class_iota[None, :]).astype(jnp.float32)
    grad_hess = jnp.concatenate(
        [
            (soft_prob - target).astype(jnp.bfloat16),
            (soft_prob * (1.0 - soft_prob)).astype(jnp.bfloat16),
        ],
        axis=1,
    )
    node_iota = jnp.arange(node_count, dtype=jnp.int32)
    node_match = node_ids[:, None] == node_iota[None, :]
    masked_rows = jnp.where(
        node_match[:, :, None], grad_hess[:, None, :], jnp.zeros((), jnp.bfloat16)
    ).reshape(rows_dev, node_count * width)
    bin_iota = jnp.arange(bin_count, dtype=jnp.int32)
    feat_block = math.gcd(feats_dev, 8)
    block_count = feats_dev // feat_block

    def make_hot(codes):
        return (
            (codes[:, :, None] == bin_iota[None, None, :])
            .astype(jnp.bfloat16)
            .reshape(rows_dev, codes.shape[1] * bin_count)
        )

    own_rows = node_count * feat_pairs * width // lax.axis_size("rows")
    groups = lax.axis_size("rows") * own_rows // width
    node_span = groups // feat_pairs

    def block_product(block):
        block_codes = lax.dynamic_slice_in_dim(bin_codes, block * feat_block, feat_block, 1)
        return lax.dot_general(
            masked_rows,
            make_hot(block_codes),
            (((0,), (0,)), ((), ())),
            preferred_element_type=jnp.float32,
        )

    stacked = lax.map(block_product, jnp.arange(block_count, dtype=jnp.int32))
    product = stacked.transpose(1, 0, 2).reshape(node_span * width, feats_dev * bin_count)
    product = product.reshape(node_span, width, feat_pairs, 2 * bin_count).transpose(0, 2, 1, 3)
    owned_hist = lax.psum_scatter(
        product.reshape(lax.axis_size("rows") * own_rows, 2 * bin_count),
        "rows",
        scatter_dimension=0,
        tiled=True,
    )
    owned = (
        owned_hist.reshape(pairs_dev // 2, width, 2, bin_count)
        .transpose(0, 2, 3, 1)
        .reshape(pairs_dev, bin_count, width)
    )
    lower_mask = (
        (bin_iota[:, None] < bin_iota[None, :]) & (bin_iota[:, None] < bin_count - 1)
    ).astype(jnp.float32)
    left_base = jnp.einsum("pbc,bt->ptc", owned, lower_mask, precision=lax.Precision.HIGHEST)
    node_total = jnp.sum(owned, axis=1, keepdims=True)
    missing_sum = owned[:, bin_count - 1 :, :]
    left_miss = left_base + missing_sum
    parent_score = split_score(node_total, classes)
    gain_left = (
        split_score(left_miss, classes)
        + split_score(node_total - left_miss, classes)
        - parent_score
    )
    gain_right = (
        split_score(left_base, classes)
        + split_score(node_total - left_base, classes)
        - parent_score
    )
    gain_rows = (jnp.concatenate([gain_left, gain_right], axis=1) / (2.0 * classes))[None]
    row_feature = jnp.sum(jnp.where(node_match, split_feature[None, :], 0), axis=1)
    row_bin = jnp.sum(jnp.where(node_match, split_bin[None, :], 0), axis=1)
    row_missing = jnp.sum(jnp.where(node_match, split_missing[None, :], 0), axis=1)
    feat_index = lax.axis_index("feat")
    local_col = row_feature - feat_index * feats_dev
    is_owned = (local_col >= 0) & (local_col < feats_dev)
    col_iota = jnp.arange(feats_dev, dtype=jnp.int32)
    row_code = jnp.sum(jnp.where(col_iota[None, :] == local_col[:, None], bin_codes, 0), axis=1)
    goes_left = (row_code < row_bin) | (row_code == bin_count - 1) & (row_missing == 1)
    right_flag = jnp.where(is_owned & jnp.logical_not(goes_left), 1.0, 0.0).astype(jnp.float32)
    side_count = lax.psum(right_flag, "feat")
    row_side = (side_count > 0.5).astype(jnp.int32)
    slot_iota = jnp.arange(2 * node_count, dtype=jnp.int32)
    slot_hot = (node_ids * 2 + row_side)[:, None] == slot_iota[None, :]
    row_index = lax.axis_index("rows")
    my_node = row_index // per_node
    base_feat = feat_index * feats_dev + row_index % per_node * pairs_dev
    local_feat = split_feature[my_node] - base_feat
    holds = ((local_feat >= 0) & (local_feat < pairs_dev)).astype(jnp.float32)
    chosen = owned[jnp.clip(local_feat, 0, pairs_dev - 1)]
    bin_mask = ((bin_iota < split_bin[my_node]) & (bin_iota < bin_count - 1)).astype(jnp.float32)
    left_sum = jnp.sum(chosen * bin_mask[:, None], axis=0) + chosen[bin_count - 1] * split_missing[
        my_node
    ].astype(jnp.float32)
    node_sum = jnp.sum(chosen, axis=0)
    entry = jnp.stack([left_sum, node_sum - left_sum], axis=0) * holds
    placed = jnp.where(
        (node_iota == my_node)[:, None, None], entry[None], jnp.zeros((), jnp.float32)
    )
    side_sums = lax.psum(placed, ("rows", "feat"))
    leaves = -side_sums[..., :classes] / (side_sums[..., classes:] + reg_lambda)
    update = jnp.dot(
        slot_hot.astype(jnp.float32),
        leaves.reshape(2 * node_count, classes),
        precision=lax.Precision.HIGHEST,
    )
    new_logits = logits + step_size * update
    return (new_logits, gain_rows, leaves)


def solution(mesh):
    return jax.shard_map(
        local,
        mesh=mesh,
        in_specs=(P("rows", None), P("rows"), P("rows"), P("rows", "feat"), P(), P(), P()),
        out_specs=(P("rows", None), P("rows", "feat", None), P()),
        check_vma=False,
    )
```

profile of v0, /device:TPU:1, one launch (start us, length us, event | category | flops | bytes accessed | tf_op | source)
XLA Modules:
  0.0 613.6 jit_solution(12515425515692365684)
XLA Ops:
  7.2 1.1 exponential_reduce_fusion
  8.3 0.7 iota_compare_fusion.4
  9.0 1.1 subtract_convert_fusion
  10.2 25.2 %while.11 = (s32[]{:T(128)}, f32[4,512,512]{1,2,0:T(8,128)}, s32[4]{0:T(128)S(1)}, s32[3072,32]{0,1:T(8,128)}, bf16[3072,64]{0,1:T(8,128)(2,1)S(1)}, /*index=5*/...) while((s32[]{:T(128)}, f32[4,512,512]{1,2,0:T(8,128)}, ...), condition=%wide.region_7.8_spmd.clone, body=%wide.region_6.7_spmd.clone.sunk | while | flops 1613758464 | bytes 11207331 | solution.py:67
  10.2 0.6 dynamic_slice.31
  11.5 0.9 constant_dynamic-slice_fusion.2
  12.4 0.9 bitcast_compare_fusion.2
  13.7 2.8 fusion.35
  17.7 0.9 constant_dynamic-slice_fusion.2
  18.7 0.9 bitcast_compare_fusion.2
  19.9 2.8 fusion.35
  22.8 0.6 dynamic_slice.31
  24.0 0.9 constant_dynamic-slice_fusion.2
  25.0 0.9 bitcast_compare_fusion.2
  26.3 2.8 fusion.35
  29.1 0.6 dynamic_slice.31
  30.3 0.9 constant_dynamic-slice_fusion.2
  31.3 0.9 bitcast_compare_fusion.2
  32.5 2.8 fusion.35
  35.4 5.4 copy.31
  40.8 5.5 reshape_reshape.3
  46.3 5.4 copy.32
  52.3 0.6 dynamic_slice.19
  53.5 0.6 dynamic_slice.21
  54.1 0.6 dynamic_slice.22
  55.6 75.7 %psum.14 = f32[3072]{0:T(1024)S(1)} all-reduce(f32[3072]{0:T(1024)S(1)} %and_select_fusion), channel_id=1, replica_groups=mesh['rows'=64,'feat'=8] {'feat'}, use_global_device_ids=true, to_apply=%region_4.5 | all-reduce | flops 3072 | bytes 24576 | tf_op jit(solution)/shard_map/psum | solution.py:110
  131.4 0.7 and_convert_fusion
  132.1 359.6 %reduce-scatter.2.cloned.1.call-done = f32[128,128]{1,0:T(8,128)} async-done(((f32[8192,128]{1,0:T(8,128)}), f32[128,128]{1,0:T(8,128)}) %reduce-scatter.2.cloned.1.call-update) | async-done | bytes 65552 | tf_op jit(solution)/shard_map/reduce_scatter | solution.py:70
  491.6 1.0 reshape.173
  493.5 110.9 %psum.15 = f32[8,2,64]{2,1,0:T(2,128)S(1)} all-reduce(f32[8,2,64]{2,1,0:T(2,128)S(1)} %broadcast_select_fusion.1), channel_id=1, replica_groups=mesh['rows'=64,'feat'=8] {'rows','feat'}, use_global_device_ids=true, to_apply=%region_11.12 | all-reduce | flops 1024 | bytes 8192 | tf_op jit(solution)/shard_map/psum | solution.py:129
  605.0 0.7 maximum_multiply_fusion
  605.6 1.1 fusion.5
  (55 shorter events, 4.3 us)
Async XLA Ops:
  7.2 484.5 %reduce-scatter.2.cloned.1.call-start = ((), (), s32[]{:S(2)}) async-start(), calls=%async_computation.1 | async-start | bytes 4259840 | tf_op jit(solution)/shard_map/reduce_scatter | solution.py:70
  51.6 0.7 copy-start.4
  51.6 1.9 copy-start.6
  51.6 2.5 copy-start.5
  51.6 3.7 copy-start.2
  51.6 3.9 copy-start.1
  51.6 554.0 %copy-start = (f32[3072,32]{0,1:T(8,128)S(1)}, f32[3072,32]{0,1:T(8,128)}, u32[]{:S(2)}) copy-start(f32[3072,32]{0,1:T(8,128)} %param.9) | copy-start | bytes 1179652
  604.5 2.2 copy-start.3
Sparse Core Ops, SparseCore 0:
  51.8 439.8 reduce-scatter.1
where the time goes:
time: 614 us
  waiting for transfers between devices  360 us (59%)
  blocking collectives  187 us (30%)
  local copies, waits for them, and re-layouts  26 us (4%)
  between operations  15.6 us (3%)
  matrix products  12.7 us (2%)
  other arithmetic  10.3 us (2%)
    reduce_scatter x1, waiting for transfers between devices, local(): lax.psum_scatter(product.reshape(lax.axis_size('rows') * own_rows, 2 * bi...  360 us
    psum x1, blocking collectives, local(): side_sums = lax.psum(placed, ('rows', 'feat'))  111 us
    psum x1, blocking collectives, local(): side_count = lax.psum(right_flag, 'feat')  75.7 us
  transfers between devices with their start and end apart: 1, of which 1 were waited for; matrix products, arithmetic and copies ran while one was open for 0% of the time, Pallas kernels for 0%

commit v1 on v0

--- a/solution.py
+++ b/solution.py
@@ -126,7 +126,9 @@
     placed = jnp.where(
         (node_iota == my_node)[:, None, None], entry[None], jnp.zeros((), jnp.float32)
     )
-    side_sums = lax.psum(placed, ("rows", "feat"))
+    side_sums = placed
+    for over in ("feat", "rows"):
+        side_sums = lax.psum(side_sums, over)
     leaves = -side_sums[..., :classes] / (side_sums[..., classes:] + reg_lambda)
     update = jnp.dot(
         slot_hot.astype(jnp.float32),

time: 614 us -> 796 us (1.30)
  blocking collectives: 187 us -> 293 us
  waiting for transfers between devices: 360 us -> 435 us
    psum x2, blocking collectives: 187 us -> 293 us  [local(): side_sums = lax.psum(side_sums, over)]
    reduce_scatter x1, waiting for transfers between devices: 360 us -> 435 us  [local(): lax.psum_scatter(product.reshape(lax.axis_size('rows') * own_rows, 2 * bi...]
where the time goes in v1:
time: 796 us
  waiting for transfers between devices  435 us (55%)
  blocking collectives  293 us (37%)
  local copies, waits for them, and re-layouts  26 us (3%)
  between operations  15.6 us (2%)
  matrix products  12.7 us (2%)
  other arithmetic  10.3 us (1%)
    reduce_scatter x1, waiting for transfers between devices, local(): lax.psum_scatter(product.reshape(lax.axis_size('rows') * own_rows, 2 * bi...  435 us
    psum x2, blocking collectives, local(): side_sums = lax.psum(side_sums, over)  293 us
  transfers between devices with their start and end apart: 1, of which 1 were waited for; matrix products, arithmetic and copies ran while one was open for 0% of the time, Pallas kernels for 0%

profile of v1, /device:TPU:1, one launch (start us, length us, event | category | flops | bytes accessed | tf_op | source)
XLA Modules:
  0.0 795.7 jit_solution(3057478180173478022)
XLA Ops:
  7.2 1.1 exponential_reduce_fusion
  8.3 0.7 iota_compare_fusion.4
  9.0 1.1 subtract_convert_fusion
  10.2 25.2 %while.11 = (s32[]{:T(128)}, f32[4,512,512]{1,2,0:T(8,128)}, s32[4]{0:T(128)S(1)}, s32[3072,32]{0,1:T(8,128)}, bf16[3072,64]{0,1:T(8,128)(2,1)S(1)}, /*index=5*/...) while((s32[]{:T(128)}, f32[4,512,512]{1,2,0:T(8,128)}, ...), condition=%wide.region_7.8_spmd.clone, body=%wide.region_6.7_spmd.clone.sunk | while | flops 1613758464 | bytes 11207331 | solution.py:67
  10.2 0.6 dynamic_slice.31
  11.5 0.9 constant_dynamic-slice_fusion.2
  12.4 0.9 bitcast_compare_fusion.2
  13.7 2.8 fusion.35
  17.7 0.9 constant_dynamic-slice_fusion.2
  18.7 0.9 bitcast_compare_fusion.2
  19.9 2.8 fusion.35
  22.8 0.6 dynamic_slice.31
  24.0 0.9 constant_dynamic-slice_fusion.2
  25.0 0.9 bitcast_compare_fusion.2
  26.3 2.8 fusion.35
  29.1 0.6 dynamic_slice.31
  30.3 0.9 constant_dynamic-slice_fusion.2
  31.3 0.9 bitcast_compare_fusion.2
  32.5 2.8 fusion.35
  35.4 5.4 copy.31
  40.8 5.5 reshape_reshape.3
  46.3 5.4 copy.32
  52.3 0.6 dynamic_slice.19
  53.5 0.6 dynamic_slice.21
  54.1 0.6 dynamic_slice.22
  55.4 0.7 and_convert_fusion
  56.3 435.1 %reduce-scatter.2.cloned.1.call-done = f32[128,128]{1,0:T(8,128)} async-done(((f32[8192,128]{1,0:T(8,128)}), f32[128,128]{1,0:T(8,128)}) %reduce-scatter.2.cloned.1.call-update) | async-done | bytes 65552 | tf_op jit(solution)/shard_map/reduce_scatter | solution.py:70
  491.4 1.0 reshape.173
  493.2 70.5 %all-reduce = (f32[8,2,64]{2,1,0:T(2,128)S(1)}, f32[3072]{0:T(1024)S(1)}) all-reduce(f32[8,2,64]{2,1,0:T(2,128)S(1)} %broadcast_select_fusion.1, f32[3072]{0:T(1024)S(1)} %and_select_fusion), channel_id=1, replica_groups=mesh['rows'=64,'feat'=8] {'feat'}, use_global_device_ids=true, to_apply=%region_11.12 | all-reduce | flops 4096 | bytes 32768 | tf_op jit(solution)/shard_map/psum | solution.py:131
  563.7 222.8 %psum.23 = f32[8,2,64]{2,1,0:T(2,128)S(1)} all-reduce(f32[8,2,64]{2,1,0:T(2,128)S(1)} %get-tuple-element.68), channel_id=1, replica_groups=mesh['rows'=64,'feat'=8] {'rows'}, use_global_device_ids=true, to_apply=%region_12.13 | all-reduce | flops 1024 | bytes 8192 | tf_op jit(solution)/shard_map/psum | solution.py:131
  787.1 0.7 maximum_multiply_fusion
  787.8 1.1 fusion.5
  (55 shorter events, 4.4 us)
Async XLA Ops:
  7.2 484.2 %reduce-scatter.2.cloned.1.call-start = ((), (), s32[]{:S(2)}) async-start(), calls=%async_computation.1 | async-start | bytes 4259840 | tf_op jit(solution)/shard_map/reduce_scatter | solution.py:70
  51.6 0.7 copy-start.4
  51.6 1.9 copy-start.6
  51.6 2.5 copy-start.5
  51.6 4.4 copy-start.2
  51.6 4.6 copy-start.1
  51.6 736.1 %copy-start = (f32[3072,32]{0,1:T(8,128)S(1)}, f32[3072,32]{0,1:T(8,128)}, u32[]{:S(2)}) copy-start(f32[3072,32]{0,1:T(8,128)} %param.9) | copy-start | bytes 1179652
  786.6 2.2 copy-start.3
Sparse Core Ops, SparseCore 0:
  51.8 439.5 reduce-scatter.1
